TPU v7x, 512 devices: a whole 4x4x16 slice. The times are simulated.
512 devices in a mesh: pix: 128 (over z_hi, x, y, core), row: 4 (over z_lo).
Axes of the slice: x: 4, y: 4, z: 16 (z_hi: 4, z_lo: 4; z = z_hi * 4 + z_lo), core: 2. Of those that a mesh axis runs over, the one named last changes fastest.
Arguments:
- band_images: bfloat16 [256, 128, 8192], P('pix', 'row'), may hold values from -6 to 6
- pivots: int32 [2, 32], replicated, may hold values from 0 to 1048575, as said below
Outputs:
- residual: bfloat16 [8192, 128, 256], P(('pix', 'row'))
- coefficients: bfloat16 [64, 8192, 128], P(None, ('pix', 'row'))
Inputs may be any that keep to these rules, and one draw needn't show every extreme that they name: All 64 pivots lie in different columns, and every group of 32 lines starting at a multiple of 32 holds at least one pivot.
All inputs are finite; a program needn't handle non-finite values.
Results may differ from a plain program's by a relative error of at most 0.001.
Values may be sent and summed in bfloat16 or wider, within the bound.
A program may use at most 192 MiB of HBM per device.

v0:
```python
import jax
import jax.numpy as jnp
from jax import lax
from jax.sharding import PartitionSpec as P

highest = lax.Precision.HIGHEST


def orthonormal(spectra):
    gram = jnp.dot(spectra, spectra.T, precision=highest)
    factor = jnp.linalg.cholesky(gram)
    return jax.scipy.linalg.solve_triangular(factor, spectra, lower=True)


def project(block, basis):
    count = basis.shape[0] // 2
    first = basis[:count]
    second = basis[count:]
    coef_one = jnp.einsum("clb,kb->kcl", block, first, precision=highest)
    remain = block - jnp.einsum("kcl,kb->clb", coef_one, first, precision=highest)
    coef_two = jnp.einsum("clb,kb->kcl", remain, second, precision=highest)
    remain = remain - jnp.einsum("kcl,kb->clb", coef_two, second, precision=highest)
    return (
        remain.astype(jnp.bfloat16),
        jnp.concatenate([coef_one, coef_two], axis=0).astype(jnp.bfloat16),
    )


def shards(band_images, pivots):
    band_dev, line_dev, cols_all = band_images.shape
    pix_count = lax.axis_size("pix")
    row_count = lax.axis_size("row")
    narrow = cols_all // (pix_count * row_count)
    flat_pivots = pivots.reshape(-1)
    line_index = flat_pivots // cols_all
    column = flat_pivots % cols_all
    offset = line_index - lax.axis_index("row") * line_dev
    inside = (offset >= 0) & (offset < line_dev)
    position = jnp.clip(offset, 0, line_dev - 1) * cols_all + column
    picked = jnp.take(band_images.reshape(band_dev, line_dev * cols_all), position, axis=1)
    picked = jnp.where(inside[None, :], picked, jnp.zeros_like(picked))
    placed = jnp.zeros((band_dev * pix_count, flat_pivots.shape[0]), jnp.float32)
    placed = lax.dynamic_update_slice_in_dim(
        placed, picked.astype(jnp.float32), lax.axis_index("pix") * band_dev, 0
    )
    spectra = lax.psum(placed, ("pix", "row"))
    basis = orthonormal(spectra.T)
    shaped = band_images.reshape(band_dev, line_dev, pix_count, row_count, narrow)
    arrived = lax.all_to_all(
        lax.all_to_all(shaped, "pix", split_axis=2, concat_axis=0, tiled=True),
        "row",
        split_axis=3,
        concat_axis=1,
        tiled=True,
    )
    block = (
        arrived.reshape(arrived.shape[0], arrived.shape[1], narrow)
        .transpose(2, 1, 0)
        .astype(jnp.float32)
    )
    return project(block, basis)


def solution(mesh):
    placed = (P("pix", "row", None), P())
    return jax.shard_map(
        shards,
        mesh=mesh,
        in_specs=placed,
        out_specs=(P(("pix", "row"), None, None), P(None, ("pix", "row"), None)),
        check_vma=False,
    )
```

profile of v0, /device:TPU:1, one launch (start us, length us, event | category | flops | bytes accessed | tf_op | source)
XLA Modules:
  0.0 625.1 jit_solution(1769854623598273289)
XLA Ops:
  7.2 4.6 copy.14
  11.7 5.6 copy.22
  17.3 6.5 %reshape.198 = bf16[128,2,2048]{2,1,0:T(2,128)(2,1)S(1)} reshape(bf16[128,2,4,16,32]{4,3,2,1,0:T(8,128)(2,1)} %bitcast.50) | data formatting | bytes 2097152
  23.8 76.3 %all_to_all.33 = bf16[128,2,2048]{2,1,0:T(2,128)(2,1)S(1)} all-to-all(bf16[128,2,2048]{2,1,0:T(2,128)(2,1)S(1)} %reshape.198), channel_id=1, replica_groups=mesh['pix'=128,'row'=4] {'pix'}, dimensions={0} | all-to-all | bytes 2097152 | tf_op jit(solution)/shard_map/all_to_all | solution.py:50
  100.1 3.5 reshape.199
  103.6 6.9 %copy.16 = bf16[256,32,1,4,16]{0,4,2,1,3:T(8,128)(2,1)} copy(bf16[256,32,1,4,16]{1,4,3,0,2:T(8,128)(2,1)} %bitcast.49) | data formatting | bytes 2097152 | tf_op jit(solution)/shard_map/all_to_all | solution.py:50
  110.6 8.3 %all-to-all-start.1 = ((bf16[256,32,1,4,16]{0,4,2,1,3:T(8,128)(2,1)}), bf16[256,32,1,4,16]{0,4,2,1,3:T(8,128)(2,1)S(1)}, u32[]{:S(2)}, u32[]{:S(2)}) async-start(bf16[256,32,1,4,16]{0,4,2,1,3:T(8,128)(2,1)} %copy.16), calls=%async_computation.1 | async-start | bytes 2097152 | tf_op jit(solution)/shard_map/all_to_all | solution.py:49
  118.8 0.0 all-reduce.2.cloned.1.call-start
  118.8 0.1 reshape.185
  118.9 0.1 reshape.187
  119.0 40.3 %copy.18 = bf16[2,32,8192]{0,2,1:T(8,128)(2,1)} copy(bf16[2,32,8192]{2,1,0:T(8,128)(2,1)S(1)} %copy-done) | data formatting | bytes 2097152 | tf_op args[0]
  159.4 1.5 gather_fusion
  160.9 0.1 convert_bitcast_fusion
  161.0 0.6 dynamic_update_slice.3
  161.6 0.0 copy-start.1
  161.6 0.6 copy-done.1
  162.3 0.0 all-reduce.2.cloned.1.call-update
  162.3 432.6 %all-reduce.2.cloned.1.call-done = f32[256,64]{0,1:T(8,128)} async-done(((f32[256,64]{0,1:T(8,128)}), f32[256,64]{0,1:T(8,128)}) %all-reduce.2.cloned.1.call-update) | async-done | bytes 65552 | tf_op jit(solution)/shard_map/psum | solution.py:46
  594.9 1.1 fusion.13
  596.0 0.1 copy.19
  596.1 5.8 cholesky.16
  602.0 0.6 compare_reduce_fusion
  602.7 0.7 fusion
  603.3 4.9 custom-call.7
  608.2 1.1 fusion.1
  609.3 0.0 all-to-all-done.1
  609.3 0.3 copy.17
  609.7 1.0 fusion.12
  610.7 1.8 convert_subtract_fusion
  612.5 2.0 fusion.11
  614.6 0.9 copy.20
  615.5 2.8 subtract_convert_fusion
  (12 shorter events, 0.1 us)
Async XLA Ops:
  110.6 8.3 %copy-start.2 = (s32[2,32]{1,0:T(2,128)S(1)}, s32[2,32]{1,0:T(2,128)}, u32[]{:S(2)}) copy-start(s32[2,32]{1,0:T(2,128)} %param.3) | copy-start | bytes 772
  110.6 8.4 %copy-start = (bf16[2,32,8192]{2,1,0:T(8,128)(2,1)S(1)}, bf16[2,32,8192]{2,1,0:T(8,128)(2,1)}, u32[]{:S(2)}) copy-start(bf16[2,32,8192]{2,1,0:T(8,128)(2,1)} %param.2) | copy-start | bytes 3145732
  110.6 498.8 %all-to-all-start.1 = ((bf16[256,32,1,4,16]{0,4,2,1,3:T(8,128)(2,1)}), bf16[256,32,1,4,16]{0,4,2,1,3:T(8,128)(2,1)S(1)}, u32[]{:S(2)}, u32[]{:S(2)}) async-start(bf16[256,32,1,4,16]{0,4,2,1,3:T(8,128)(2,1)} %copy.16), calls=%async_computation.1 | async-start | bytes 2097152 | tf_op jit(solution)/shard_map/all_to_all | solution.py:49
  118.8 476.1 %all-reduce.2.cloned.1.call-start = ((), (), s32[]{:S(2)}) async-start(), calls=%async_computation.2 | async-start | bytes 131072 | tf_op jit(solution)/shard_map/psum | solution.py:46
  161.6 0.6 copy-start.1
Sparse Core Ops, SparseCore 0:
  162.4 432.4 all-reduce.1
where the time goes:
time: 626 us; the launch traced here: 625 us
  waiting for transfers between devices  433 us (69%)
  blocking collectives  76.3 us (12%)
  local copies, waits for them, and re-layouts  71.7 us (11%)
  between operations  14.2 us (2%)
  other arithmetic  12.2 us (2%)
  matrix products  9.87 us (2%)
  starting transfers between devices  8.26 us (1%)
    psum x1, waiting for transfers between devices, shards(): spectra = lax.psum(placed, ('pix', 'row'))  433 us
    all_to_all x1, blocking collectives, shards(): lax.all_to_all(shaped, 'pix', split_axis=2, concat_axis=0, tiled=True)  76.3 us
    unnamed x11, local copies, waits for them, and re-layouts  56.5 us
  transfers between devices with their start and end apart: 2, of which 1 were waited for; matrix products, arithmetic and copies ran while one was open for 9% of the time, Pallas kernels for 0%

commit v1 on v0

--- a/solution.py
+++ b/solution.py
@@ -43,7 +43,7 @@
     placed = lax.dynamic_update_slice_in_dim(
         placed, picked.astype(jnp.float32), lax.axis_index("pix") * band_dev, 0
     )
-    spectra = lax.psum(placed, ("pix", "row"))
+    spectra = lax.psum(lax.psum(placed, "pix"), "row")
     basis = orthonormal(spectra.T)
     shaped = band_images.reshape(band_dev, line_dev, pix_count, row_count, narrow)
     arrived = lax.all_to_all(

time: 626 us -> 1650 us (2.64)
  waiting for transfers between devices: 433 us -> 1450 us
    psum x1 -> x2, waiting for transfers between devices: 433 us -> 1450 us  [shards(): spectra = lax.psum(lax.psum(placed, 'pix'), 'row')]
  transfers between devices with their start and end apart: 2 -> 3, of which waited for: 1 -> 2; matrix products, arithmetic and copies ran while one was open for 9% -> 3% of each run, Pallas kernels for 0% -> 0%
where the time goes in v1:
time: 1650 us; the launch traced here: 1640 us
  waiting for transfers between devices  1450 us (88%)
  blocking collectives  76.3 us (5%)
  local copies, waits for them, and re-layouts  71.7 us (4%)
    psum x2, waiting for transfers between devices, shards(): spectra = lax.psum(lax.psum(placed, 'pix'), 'row')  1450 us
    all_to_all x1, blocking collectives, shards(): lax.all_to_all(shaped, 'pix', split_axis=2, concat_axis=0, tiled=True)  76.3 us
    unnamed x11, local copies, waits for them, and re-layouts  56.5 us
  transfers between devices with their start and end apart: 3, of which 2 were waited for; matrix products, arithmetic and copies ran while one was open for 3% of the time, Pallas kernels for 0%

profile of v1, /device:TPU:1, one launch (start us, length us, event | category | flops | bytes accessed | tf_op | source)
XLA Modules:
  0.0 1643.9 jit_solution(8395051416021219381)
XLA Ops:
  7.2 4.6 copy.14
  11.7 5.6 copy.22
  17.3 6.5 reshape.198
  23.8 76.3 %all_to_all.33 = bf16[128,2,2048]{2,1,0:T(2,128)(2,1)S(1)} all-to-all(bf16[128,2,2048]{2,1,0:T(2,128)(2,1)S(1)} %reshape.198), channel_id=1, replica_groups=mesh['pix'=128,'row'=4] {'pix'}, dimensions={0} | all-to-all | bytes 2097152 | tf_op jit(solution)/shard_map/all_to_all | solution.py:50
  100.1 3.5 reshape.199
  103.6 6.9 copy.16
  110.6 8.3 all-to-all-start.1
  118.8 0.1 reshape.185
  118.9 0.1 reshape.187
  119.0 40.3 %copy.18 = bf16[2,32,8192]{0,2,1:T(8,128)(2,1)} copy(bf16[2,32,8192]{2,1,0:T(8,128)(2,1)S(1)} %copy-done) | data formatting | bytes 2097152 | tf_op args[0]
  159.4 1.5 gather_fusion
  160.9 0.1 convert_bitcast_fusion
  161.0 0.6 dynamic_update_slice.3
  161.6 0.6 copy-done.1
  162.3 0.0 all-reduce.3.cloned.1.call-update
  162.3 0.2 all-reduce.5.cloned.1.call-start
  162.5 1394.6 %all-reduce.3.cloned.1.call-done = f32[256,64]{0,1:T(8,128)} async-done(((f32[256,64]{0,1:T(8,128)}), f32[256,64]{0,1:T(8,128)}) %all-reduce.3.cloned.1.call-update) | async-done | bytes 65552 | tf_op jit(solution)/shard_map/psum | solution.py:46
  1557.2 0.0 all-reduce.5.cloned.1.call-update
  1557.2 56.5 %all-reduce.5.cloned.1.call-done = f32[256,64]{0,1:T(8,128)} async-done(((f32[256,64]{0,1:T(8,128)}), f32[256,64]{0,1:T(8,128)}) %all-reduce.5.cloned.1.call-update) | async-done | bytes 65552 | tf_op jit(solution)/shard_map/psum | solution.py:46
  1613.7 1.1 fusion.13
  1614.8 0.1 copy.19
  1614.9 5.8 cholesky.16
  1620.8 0.6 compare_reduce_fusion
  1621.4 0.7 fusion
  1622.1 4.9 custom-call.7
  1627.0 1.1 fusion.1
  1628.1 0.3 copy.17
  1628.5 1.0 fusion.12
  1629.5 1.8 convert_subtract_fusion
  1631.3 2.0 fusion.11
  1633.4 0.9 copy.20
  1634.2 2.8 subtract_convert_fusion
  (15 shorter events, 0.1 us)
Async XLA Ops:
  110.6 8.3 copy-start.2
  110.6 8.4 copy-start
  110.6 1517.6 %all-to-all-start.1 = ((bf16[256,32,1,4,16]{0,4,2,1,3:T(8,128)(2,1)}), bf16[256,32,1,4,16]{0,4,2,1,3:T(8,128)(2,1)S(1)}, u32[]{:S(2)}, u32[]{:S(2)}) async-start(bf16[256,32,1,4,16]{0,4,2,1,3:T(8,128)(2,1)} %copy.16), calls=%async_computation.1 | async-start | bytes 2097152 | tf_op jit(solution)/shard_map/all_to_all | solution.py:49
  118.8 1438.3 %all-reduce.3.cloned.1.call-start = ((), (), s32[]{:S(2)}) async-start(), calls=%async_computation.2 | async-start | bytes 131072 | tf_op jit(solution)/shard_map/psum | solution.py:46
  161.6 0.6 copy-start.1
  162.3 1451.4 %all-reduce.5.cloned.1.call-start = ((), (), s32[]{:S(2)}) async-start(), calls=%async_computation.3 | async-start | bytes 131072 | tf_op jit(solution)/shard_map/psum | solution.py:46
Sparse Core Ops, SparseCore 0:
  162.4 1394.7 all-reduce.2
  1560.3 53.3 all-reduce.4

commit v2 on v0

--- a/solution.py
+++ b/solution.py
@@ -43,7 +43,7 @@
     placed = lax.dynamic_update_slice_in_dim(
         placed, picked.astype(jnp.float32), lax.axis_index("pix") * band_dev, 0
     )
-    spectra = lax.psum(placed, ("pix", "row"))
+    spectra = jnp.sum(lax.all_gather(placed, ("pix", "row")), axis=0)
     basis = orthonormal(spectra.T)
     shaped = band_images.reshape(band_dev, line_dev, pix_count, row_count, narrow)
     arrived = lax.all_to_all(

time: 626 us -> 1610 us (2.57); the launches traced: 625 us -> 1580 us
  waiting for transfers between devices: 433 us -> 1350 us
  blocking collectives: 76.3 us -> 111 us
    all_gather x0 -> x1, waiting for transfers between devices: none -> 1350 us  [shards(): spectra = jnp.sum(lax.all_gather(placed, ('pix', 'row')), axis=0)]
    psum x1 -> x0, waiting for transfers between devices: 433 us -> none  [shards(): spectra = lax.psum(placed, ('pix', 'row'))]
    all_to_all x0 -> x1, blocking collectives: none -> 35.3 us  [shards(): lax.all_to_all(lax.all_to_all(shaped, 'pix', split_axis=2, concat_axis=0,...]
    unnamed x11 -> x9, local copies, waits for them, and re-layouts: 56.5 us -> 56 us
  transfers between devices with their start and end apart: 2 -> 1, of which waited for: 1 -> 1; matrix products, arithmetic and copies ran while one was open for 9% -> 2% of each run, Pallas kernels for 0% -> 0%
where the time goes in v2:
time: 1610 us; the launch traced here: 1580 us
  waiting for transfers between devices  1350 us (84%)
  blocking collectives  111 us (7%)
  local copies, waits for them, and re-layouts  71.9 us (4%)
  other arithmetic  25.1 us (2%)
    all_gather x1, waiting for transfers between devices, shards(): spectra = jnp.sum(lax.all_gather(placed, ('pix', 'row')), axis=0)  1350 us
    all_to_all x1, blocking collectives, shards(): lax.all_to_all(shaped, 'pix', split_axis=2, concat_axis=0, tiled=True)  76.1 us
    unnamed x9, local copies, waits for them, and re-layouts  56 us
    all_to_all x1, blocking collectives, shards(): lax.all_to_all(lax.all_to_all(shaped, 'pix', split_axis=2, concat_axis=0,...  35.3 us
  transfers between devices with their start and end apart: 1, of which 1 were waited for; matrix products, arithmetic and copies ran while one was open for 2% of the time, Pallas kernels for 0%

profile of v2, /device:TPU:1, one launch (start us, length us, event | category | flops | bytes accessed | tf_op | source)
XLA Modules:
  0.0 1581.2 jit_solution(17825714756841806432)
XLA Ops:
  7.2 0.0 all-gather.2.cloned.1.call-start
  7.2 0.8 reshape.241
  8.0 0.8 reshape.243
  8.8 41.2 %copy.29 = bf16[2,32,8192]{0,2,1:T(8,128)(2,1)} copy(bf16[2,32,8192]{2,1,0:T(8,128)(2,1)} %param.2) | data formatting | bytes 2097152 | tf_op args[0]
  50.1 1.5 gather_fusion
  51.6 0.1 copy.30
  51.7 0.1 copy.31
  51.8 0.6 dynamic_update_slice.4
  52.4 0.6 copy-done.1
  53.0 0.0 all-gather.2.cloned.1.call-update
  53.1 3.1 copy.25
  56.2 5.5 copy.35
  61.7 6.5 reshape.254
  68.3 76.1 %all_to_all.33 = bf16[128,2,2048]{2,1,0:T(2,128)(2,1)S(1)} all-to-all(bf16[128,2,2048]{2,1,0:T(2,128)(2,1)S(1)} %reshape.254), channel_id=1, replica_groups=mesh['pix'=128,'row'=4] {'pix'}, dimensions={0} | all-to-all | bytes 2097152 | tf_op jit(solution)/shard_map/all_to_all | solution.py:50
  144.4 3.5 reshape.255
  147.9 6.1 copy.27
  154.1 35.3 %all_to_all.34 = bf16[256,32,1,4,16]{0,4,2,1,3:T(8,128)(2,1)S(1)} all-to-all(bf16[256,32,1,4,16]{0,4,2,1,3:T(8,128)(2,1)S(1)} %copy.27), channel_id=1, replica_groups=mesh['pix'=128,'row'=4] {'row'}, dimensions={3} | all-to-all | bytes 2097152 | tf_op jit(solution)/shard_map/all_to_all | solution.py:49
  189.4 0.3 copy.28
  189.8 1350.5 %all-gather.2.cloned.1.call-done = f32[512,256,64]{1,2,0:T(8,128)} async-done(((f32[1,256,64]{1,2,0:T(8,128)}), f32[512,256,64]{1,2,0:T(8,128)}) %all-gather.2.cloned.1.call-update) | async-done | bytes 33554448 | tf_op jit(solution)/shard_map/all_gather | solution.py:46
  1540.2 12.9 reduce_sum.9
  1553.2 0.2 fusion.14
  1553.4 0.1 copy.32
  1553.5 5.8 cholesky.16
  1559.3 0.6 compare_reduce_fusion
  1560.0 0.7 fusion
  1560.6 4.9 custom-call.7
  1565.5 0.3 fusion.1
  1565.8 1.0 fusion.13
  1566.8 1.8 convert_subtract_fusion
  1568.7 2.0 fusion.12
  1570.7 0.9 copy.33
  1571.6 2.8 subtract_convert_fusion
  (12 shorter events, 0.1 us)
Async XLA Ops:
  7.2 1533.1 %all-gather.2.cloned.1.call-start = ((), (), s32[]{:S(2)}) async-start(), calls=%async_computation.2 | async-start | bytes 33619968 | tf_op jit(solution)/shard_map/all_gather | solution.py:46
  8.8 44.2 %copy-start = (bf16[2,32,8192]{2,1,0:T(8,128)(2,1)S(1)}, bf16[2,32,8192]{2,1,0:T(8,128)(2,1)}, u32[]{:S(2)}) copy-start(bf16[2,32,8192]{2,1,0:T(8,128)(2,1)} %param.2) | copy-start | bytes 3145732
  52.4 0.6 copy-start.1
Sparse Core Ops, SparseCore 0:
  53.2 1487.0 all-gather.1
